TPU v7x, 32 devices: a whole 2x2x4 slice. The times are simulated.
32 devices in a mesh: gx: 4 (over y, core), gy: 8 (over z, x).
Axes of the slice: x: 2, y: 2, z: 4, core: 2. Of those that a mesh axis runs over, the one named last changes fastest.
Arguments:
- tokens: bfloat16 [256, 8192], P('gy', 'gx'), may hold values from -12 to 12
- w_gate: bfloat16 [8192, 28672], P('gx', 'gy'), may hold values from -0.0625 to 0.0625
- w_up: bfloat16 [8192, 28672], P('gx', 'gy'), may hold values from -0.0625 to 0.0625
- w_down: bfloat16 [28672, 8192], P('gy', 'gx'), may hold values from -0.03125 to 0.03125
- w_head: bfloat16 [8192, 1024], P('gx'), may hold values from -0.0625 to 0.0625
- partner: int32 [256], replicated, may hold values from 0 to 255, as said below
Outputs:
- block_out: bfloat16 [256, 8192], P('gy', 'gx')
- pair_loss: float32 [], replicated
- grad_gate: bfloat16 [8192, 28672], P('gx', 'gy')
- grad_up: bfloat16 [8192, 28672], P('gx', 'gy')
- grad_down: bfloat16 [28672, 8192], P('gy', 'gx')
- grad_head: bfloat16 [8192, 1024], P('gx', 'gy')
Inputs may be any that keep to these rules, and one draw needn't show every extreme that they name: partner[i] differs from i, and every token is the partner of exactly one token.
All inputs are finite; a program needn't handle non-finite values.
Results may differ from a plain program's by a relative error of at most 0.029.
Values may be sent and summed in bfloat16 or wider, within the bound.
A program may use at most 256 MiB of HBM per device.

v0:
```python
import math
import jax
import jax.numpy as jnp
from jax import lax
from jax.sharding import PartitionSpec as P


def contract_lead(left_mat, right_mat):
    return lax.dot_general(
        left_mat, right_mat, (((0,), (0,)), ((), ())), preferred_element_type=jnp.float32
    )


def contract_last(left_mat, right_mat):
    return lax.dot_general(
        left_mat, right_mat, (((1,), (1,)), ((), ())), preferred_element_type=jnp.float32
    )


def score_rows(proj_all, partner, row_count, score_scale):
    token_count = proj_all.shape[0]
    scores = contract_last(proj_all, proj_all) * score_scale
    row_ids = jnp.arange(row_count, dtype=jnp.int32)
    col_ids = jnp.arange(token_count, dtype=jnp.int32)
    scores = jnp.where(row_ids[:, None] == col_ids[None, :], -jnp.inf, scores)
    row_max = jnp.max(scores, axis=1, keepdims=True)
    log_total = row_max[:, 0] + jnp.log(jnp.sum(jnp.exp(scores - row_max), axis=1))
    is_partner = col_ids[None, :] == partner[:, None]
    positive = jnp.sum(jnp.where(is_partner, scores, 0.0), axis=1)
    weights_grad = (jnp.exp(scores - log_total[:, None]) - is_partner.astype(jnp.float32)).astype(
        jnp.bfloat16
    )
    return (weights_grad, log_total - positive)


def per_device(tokens, w_gate, w_up, w_down, w_head, partner):
    tok_share = tokens.shape[0]
    head_width = w_head.shape[1]
    score_scale = 1.0 / math.sqrt(head_width)
    rows_all = lax.all_gather(tokens, "gy", axis=0, tiled=True)
    token_count = rows_all.shape[0]
    row_share = token_count // lax.axis_size("gx")
    x_first = lax.axis_index("gx") * row_share
    gate_all, up_all = (
        lax.psum(
            jnp.dot(rows_all, w_gate, preferred_element_type=jnp.float32).astype(jnp.bfloat16), "gx"
        ).astype(jnp.float32),
        lax.psum(
            jnp.dot(rows_all, w_up, preferred_element_type=jnp.float32).astype(jnp.bfloat16), "gx"
        ).astype(jnp.float32),
    )
    hidden_all = (gate_all * jax.nn.sigmoid(gate_all) * up_all).astype(jnp.bfloat16)
    gate_mine = lax.dynamic_slice_in_dim(gate_all, x_first, row_share, 0)
    up_mine = lax.dynamic_slice_in_dim(up_all, x_first, row_share, 0)
    picked = hidden_all
    down_out = lax.psum_scatter(
        jnp.dot(picked, w_down, preferred_element_type=jnp.float32).astype(jnp.bfloat16),
        "gy",
        scatter_dimension=0,
        tiled=True,
    ).astype(jnp.float32)
    block_out = (tokens.astype(jnp.float32) + down_out).astype(jnp.bfloat16)
    projected = lax.psum(
        jnp.dot(block_out, w_head, preferred_element_type=jnp.float32).astype(jnp.bfloat16), "gx"
    )
    proj_all = lax.all_gather(projected, "gy", axis=0, tiled=True)
    first_row = lax.axis_index("gy") * tok_share
    weights_all, row_loss = score_rows(proj_all, partner, token_count, score_scale)
    mine_rows = lax.dynamic_slice_in_dim(weights_all, first_row, tok_share, 0)
    mine_cols = lax.dynamic_slice_in_dim(weights_all, first_row, tok_share, 1)
    row_part = jnp.dot(mine_rows, proj_all, preferred_element_type=jnp.float32)
    column_part = contract_lead(mine_cols, proj_all)
    pair_loss = jnp.sum(row_loss) / token_count
    grad_proj = ((row_part + column_part) * score_scale).astype(jnp.bfloat16)
    grad_block = contract_last(grad_proj, w_head).astype(jnp.bfloat16)
    grad_head = lax.psum_scatter(
        contract_lead(block_out, grad_proj).astype(jnp.bfloat16),
        "gy",
        scatter_dimension=1,
        tiled=True,
    )
    block_grads = lax.all_gather(grad_block, "gy", axis=0, tiled=True)
    grad_down = contract_lead(hidden_all, block_grads).astype(jnp.bfloat16)
    picked = block_grads
    grad_hidden = lax.psum_scatter(
        contract_last(picked, w_down).astype(jnp.bfloat16), "gx", scatter_dimension=0, tiled=True
    ).astype(jnp.float32)
    sigmoid_gate = jax.nn.sigmoid(gate_mine)
    grad_gate_pre = (
        grad_hidden * up_mine * sigmoid_gate * (1.0 + gate_mine * (1.0 - sigmoid_gate))
    ).astype(jnp.bfloat16)
    grad_up_pre = (grad_hidden * gate_mine * sigmoid_gate).astype(jnp.bfloat16)
    gate_grads, up_grads = (
        lax.all_gather(grad_gate_pre, "gx", axis=0, tiled=True),
        lax.all_gather(grad_up_pre, "gx", axis=0, tiled=True),
    )
    grad_gate = contract_lead(rows_all, gate_grads).astype(jnp.bfloat16)
    grad_up = contract_lead(rows_all, up_grads).astype(jnp.bfloat16)
    return (block_out, pair_loss, grad_gate, grad_up, grad_down, grad_head)


def solution(mesh):
    in_specs = (P("gy", "gx"), P("gx", "gy"), P("gx", "gy"), P("gy", "gx"), P("gx", None), P())
    out_specs = (P("gy", "gx"), P(), P("gx", "gy"), P("gx", "gy"), P("gy", "gx"), P("gx", "gy"))
    return jax.shard_map(
        per_device, mesh=mesh, in_specs=in_specs, out_specs=out_specs, check_vma=False
    )
```

profile of v0, /device:TPU:0, one launch (start us, length us, event | category | flops | bytes accessed | tf_op | source)
XLA Modules:
  0.0 527.0 jit_solution(3588408594306243018)
XLA Ops:
  7.9 45.1 %all-gather.5.cloned.1.call-done = bf16[256,2048]{1,0:T(8,128)(2,1)} async-done(((bf16[32,2048]{1,0:T(8,128)(2,1)}), bf16[256,2048]{1,0:T(8,128)(2,1)}) %all-gather.5.cloned.1.call-update) | async-done | bytes 1048592 | tf_op jit(solution)/shard_map/all_gather | solution.py:40
  53.0 10.8 %convolution_convert_fusion.4 = bf16[256,3584]{1,0:T(8,128)(2,1)} fusion(bf16[256,2048]{1,0:T(8,128)(2,1)} %all-gather.5.cloned.1.call-done, bf16[2048,3584]{1,0:T(8,128)(2,1)} %param.8), kind=kOutput, calls=%fused_computation.6 | convolution fusion | flops 3759013888 | bytes 17563648 | tf_op jit(solution)/shard_map/dot_general | solution.py:49
  63.8 10.3 %convolution_convert_fusion.5 = bf16[256,3584]{1,0:T(8,128)(2,1)} fusion(bf16[256,2048]{1,0:T(8,128)(2,1)S(1)} %copy-done, bf16[2048,3584]{1,0:T(8,128)(2,1)} %param.7), kind=kOutput, calls=%fused_computation.7 | convolution fusion | flops 3759013888 | bytes 17563648 | tf_op jit(solution)/shard_map/dot_general | solution.py:46
  74.1 76.0 %all-reduce.6.cloned.1.call-done = (bf16[256,3584]{1,0:T(8,128)(2,1)}, bf16[256,3584]{1,0:T(8,128)(2,1)}) async-done(((bf16[256,3584]{1,0:T(8,128)(2,1)}, bf16[256,3584]{1,0:T(8,128)(2,1)}), (bf16[256,3584]{1,0:T(8,128)(2,1)}, bf16[256,3584]{1,0:T(8,128)(2,1)})) %all-reduce.6.cloned.1.call-update) | async-done | bytes 3670032 | tf_op jit(solution)/shard_map/psum | solution.py:48
  150.1 11.6 %convolution_convert_fusion.7 = bf16[256,2048]{1,0:T(8,128)(2,1)} fusion(bf16[3584,2048]{1,0:T(8,128)(2,1)} %param.9, bf16[256,3584]{1,0:T(8,128)(2,1)} %get-tuple-element.20, bf16[256,3584]{1,0:T(8,128)(2,1)} %get-tuple-element.21), kind=kOutput, calls=%fused_computation.10 | convolution fusion | flops 3765960704 | bytes 19398656 | tf_op jit(solution)/shard_map/dot_general | solution.py:57
  161.8 63.7 %reduce-scatter.6.cloned.1.call-done = bf16[32,2048]{1,0:T(8,128)(2,1)} async-done(((bf16[256,2048]{1,0:T(8,128)(2,1)}), bf16[32,2048]{1,0:T(8,128)(2,1)}) %reduce-scatter.6.cloned.1.call-update) | async-done | bytes 131088 | tf_op jit(solution)/shard_map/reduce_scatter | solution.py:56
  226.5 3.7 convolution_convert_fusion.9
  230.2 30.1 %all-reduce.4.cloned.1.call-done = bf16[32,1024]{1,0:T(8,128)(2,1)} async-done(((bf16[32,1024]{1,0:T(8,128)(2,1)}), bf16[32,1024]{1,0:T(8,128)(2,1)}) %all-reduce.4.cloned.1.call-update) | async-done | bytes 65552 | tf_op jit(solution)/shard_map/psum | solution.py:63
  260.4 31.6 %all_gather.16 = bf16[256,1024]{1,0:T(8,128)(2,1)S(1)} all-gather(bf16[32,1024]{1,0:T(8,128)(2,1)} %all-reduce.4.cloned.1.call-done), channel_id=1, replica_groups=mesh['gx'=4,'gy'=8] {'gy'}, dimensions={0}, use_global_device_ids=true | all-gather | bytes 589824 | tf_op jit(solution)/shard_map/all_gather | solution.py:66
  293.6 4.2 convolution_convert_fusion.8
  298.0 40.0 %all-gather.7.cloned.1.call-done = bf16[256,2048]{1,0:T(8,128)(2,1)} async-done(((bf16[32,2048]{1,0:T(8,128)(2,1)}), bf16[256,2048]{1,0:T(8,128)(2,1)}) %all-gather.7.cloned.1.call-update) | async-done | bytes 1048592 | tf_op jit(solution)/shard_map/all_gather | solution.py:82
  338.0 10.7 %convolution_convert_fusion.3 = bf16[256,3584]{1,0:T(8,128)(2,1)} fusion(bf16[256,2048]{1,0:T(8,128)(2,1)} %all-gather.7.cloned.1.call-done, bf16[3584,2048]{1,0:T(8,128)(2,1)} %param.9), kind=kOutput, calls=%fused_computation.5 | convolution fusion | flops 3759013888 | bytes 17563648 | tf_op jit(solution)/shard_map/dot_general | solution.py:15
  348.8 3.9 convert_element_type.74
  352.7 2.3 convert_element_type.76
  355.0 22.5 %reduce-scatter.8.cloned.1.call-done = bf16[64,3584]{1,0:T(8,128)(2,1)} async-done(((bf16[256,3584]{1,0:T(8,128)(2,1)}), bf16[64,3584]{1,0:T(8,128)(2,1)}) %reduce-scatter.8.cloned.1.call-update) | async-done | bytes 458768 | tf_op jit(solution)/shard_map/reduce_scatter | solution.py:85
  377.5 2.9 fusion.9
  381.3 3.3 convolution_convert_fusion.6
  384.5 6.5 %copy.16 = bf16[2048,1024]{0,1:T(8,128)(2,1)} copy(bf16[2048,1024]{1,0:T(8,128)(2,1)} %convolution_convert_fusion.6) | data formatting | bytes 8388608
  391.7 11.7 %convolution_convert_fusion = bf16[3584,2048]{1,0:T(8,128)(2,1)} fusion(bf16[256,2048]{1,0:T(8,128)(2,1)} %all-gather.7.cloned.1.call-done, bf16[256,3584]{1,0:T(8,128)(2,1)S(1)} %copy-done.1, bf16[256,3584]{1,0:T(8,128)(2,1)} %get-tuple-element.21), kind=kOutput, calls=%fused_computation | convolution fusion | flops 3772776448 | bytes 19398656 | tf_op jit(solution)/shard_map/dot_general | solution.py:9
  403.5 9.1 %fusion = bf16[2048,3584]{0,1:T(8,128)(2,1)} fusion(bf16[256,3584]{1,0:T(8,128)(2,1)} %all-gather.9.cloned.1.call-done, bf16[256,2048]{1,0:T(8,128)(2,1)S(1)} %copy-done), kind=kOutput, calls=%fused_computation.3 | convolution fusion | flops 3765436416 | bytes 17563648 | tf_op jit(solution)/shard_map/dot_general | solution.py:9
  412.5 18.7 %copy.14 = bf16[2048,3584]{1,0:T(8,128)(2,1)} copy(bf16[2048,3584]{0,1:T(8,128)(2,1)} %fusion) | data formatting | bytes 29360128
  431.2 8.8 %fusion.1 = bf16[2048,3584]{0,1:T(8,128)(2,1)} fusion(bf16[256,3584]{1,0:T(8,128)(2,1)} %all-gather.11.cloned.1.call-done, bf16[256,2048]{1,0:T(8,128)(2,1)S(1)} %copy-done), kind=kOutput, calls=%fused_computation.4 | convolution fusion | flops 3765436416 | bytes 17563648 | tf_op jit(solution)/shard_map/dot_general | solution.py:9
  440.0 18.8 %copy.15 = bf16[2048,3584]{1,0:T(8,128)(2,1)} copy(bf16[2048,3584]{0,1:T(8,128)(2,1)} %fusion.1) | data formatting | bytes 29360128
  458.7 58.6 %reduce-scatter.10.cloned.1.call-done = bf16[128,2048]{1,0:T(8,128)(2,1)} async-done(((bf16[1024,2048]{1,0:T(8,128)(2,1)}), bf16[128,2048]{1,0:T(8,128)(2,1)}) %reduce-scatter.10.cloned.1.call-update) | async-done | bytes 524304
  (38 shorter events, 6.7 us)
Async XLA Ops:
  7.2 45.8 %all-gather.5.cloned.1.call-start = ((), (), s32[]{:S(2)}) async-start(), calls=%async_computation.3 | async-start | bytes 1179648 | tf_op jit(solution)/shard_map/all_gather | solution.py:40
  7.9 142.2 %all-reduce.6.cloned.1.call-start = ((), (), s32[]{:S(2)}) async-start(), calls=%async_computation.11 | async-start | bytes 7340032 | tf_op jit(solution)/shard_map/psum | solution.py:48
  53.0 10.8 %copy-start = (bf16[256,2048]{1,0:T(8,128)(2,1)S(1)}, bf16[256,2048]{1,0:T(8,128)(2,1)}, u32[]{:S(2)}) copy-start(bf16[256,2048]{1,0:T(8,128)(2,1)} %all-gather.5.cloned.1.call-done) | copy-start | bytes 3145732
  74.1 151.5 %reduce-scatter.6.cloned.1.call-start = ((), (), s32[]{:S(2)}) async-start(), calls=%async_computation.4 | async-start | bytes 1179648 | tf_op jit(solution)/shard_map/reduce_scatter | solution.py:56
  150.1 75.4 %copy-start.3 = (bf16[32,2048]{1,0:T(8,128)(2,1)S(1)}, bf16[32,2048]{1,0:T(8,128)(2,1)}, u32[]{:S(2)}) copy-start(bf16[32,2048]{1,0:T(8,128)(2,1)} %param.6) | copy-start | bytes 393220
  161.7 130.6 %copy-start.4 = (s32[256]{0:T(256)S(1)}, s32[256]{0:T(256)}, u32[]{:S(2)}) copy-start(s32[256]{0:T(256)} %param.11) | copy-start | bytes 3076
  161.8 98.6 %all-reduce.4.cloned.1.call-start = ((), (), s32[]{:S(2)}) async-start(), calls=%async_computation.5 | async-start | bytes 131072 | tf_op jit(solution)/shard_map/psum | solution.py:63
  226.5 154.8 %copy-start.2 = (bf16[32,2048]{1,0:T(8,128)(2,1)}, bf16[32,2048]{1,0:T(8,128)(2,1)S(1)}, u32[]{:S(2)}) copy-start(bf16[32,2048]{1,0:T(8,128)(2,1)S(1)} %add_convert_fusion) | copy-start | bytes 393220
  230.2 107.9 %all-gather.7.cloned.1.call-start = ((), (), s32[]{:S(2)}) async-start(), calls=%async_computation.6 | async-start | bytes 1179648 | tf_op jit(solution)/shard_map/all_gather | solution.py:82
  297.8 79.7 %reduce-scatter.8.cloned.1.call-start = ((), (), s32[]{:S(2)}) async-start(), calls=%async_computation.7 | async-start | bytes 2293760 | tf_op jit(solution)/shard_map/reduce_scatter | solution.py:85
  348.8 4.0 copy-start.1
  348.8 54.7 %all-gather.9.cloned.1.call-start = ((), (), s32[]{:S(2)}) async-start(), calls=%async_computation.8 | async-start | bytes 2293760 | tf_op jit(solution)/shard_map/all_gather | solution.py:94
  380.4 50.7 %all-gather.11.cloned.1.call-start = ((), (), s32[]{:S(2)}) async-start(), calls=%async_computation.9 | async-start | bytes 2293760 | tf_op jit(solution)/shard_map/all_gather | solution.py:95
  381.2 136.1 %reduce-scatter.10.cloned.1.call-start = ((), (), s32[]{:S(2)}) async-start(), calls=%async_computation.10 | async-start | bytes 4718592
Sparse Core Ops, SparseCore 0:
  10.1 42.8 all-gather.4
  74.2 75.9 all-reduce.5
  161.9 63.6 reduce-scatter.5
  230.3 30.0 all-reduce.3
  297.9 40.0 all-gather.6
  348.9 28.5 reduce-scatter.7
  380.6 21.1 all-gather.8
  403.9 21.1 all-gather.10
  429.2 88.0 reduce-scatter.9
where the time goes:
time: 528 us; the launch traced here: 527 us
  waiting for transfers between devices  337 us (64%)
  matrix products  84.9 us (16%)
  local copies, waits for them, and re-layouts  46 us (9%)
  blocking collectives  31.6 us (6%)
  between operations  15.7 us (3%)
  other arithmetic  10.8 us (2%)
    psum x1, waiting for transfers between devices, per_device(): lax.psum(jnp.dot(rows_all, w_up, preferred_element_type=jnp.float32).asty...  76 us
    reduce_scatter x1, waiting for transfers between devices, per_device(): lax.psum_scatter(jnp.dot(picked, w_down, preferred_element_type=jnp.float...  63.7 us
    unnamed x10, waiting for transfers between devices  60 us
    unnamed x14, local copies, waits for them, and re-layouts  46 us
    all_gather x1, waiting for transfers between devices, per_device(): rows_all = lax.all_gather(tokens, 'gy', axis=0, tiled=True)  45.1 us
    all_gather x1, waiting for transfers between devices, per_device(): block_grads = lax.all_gather(grad_block, 'gy', axis=0, tiled=True)  40 us
    dot_general x5, matrix products, contract_lead(): lax.dot_general(left_mat, right_mat, (((0,), (0,)), ((), ())), preferred_...  33.1 us
    all_gather x1, blocking collectives, per_device(): proj_all = lax.all_gather(projected, 'gy', axis=0, tiled=True)  31.6 us
  transfers between devices with their start and end apart: 9, of which 7 were waited for; matrix products, arithmetic and copies ran while one was open for 16% of the time, Pallas kernels for 0%

commit v1 on v0

--- a/solution.py
+++ b/solution.py
@@ -79,7 +79,12 @@
         scatter_dimension=1,
         tiled=True,
     )
-    block_grads = lax.all_gather(grad_block, "gy", axis=0, tiled=True)
+    ring = [grad_block]
+    for hop in range(7):
+        ring.append(lax.ppermute(ring[-1], "gy", [(dev, (dev + 1) % 8) for dev in range(8)]))
+    block_grads = jnp.roll(
+        jnp.concatenate(ring[::-1], axis=0), (lax.axis_index("gy") + 1) * ring[0].shape[0], axis=0
+    )
     grad_down = contract_lead(hidden_all, block_grads).astype(jnp.bfloat16)
     picked = block_grads
     grad_hidden = lax.psum_scatter(

time: 528 us -> 551 us (1.044)
  waiting for transfers between devices: 337 us -> 348 us
  local copies, waits for them, and re-layouts: 46 us -> 56.6 us
    ppermute x0 -> x7, waiting for transfers between devices: none -> 53.2 us  [per_device(): lax.ppermute(ring[-1], 'gy', [(dev, (dev + 1) % 8) for dev in range(8)])]
    all_gather x1 -> x0, waiting for transfers between devices: 40 us -> none  [per_device(): block_grads = lax.all_gather(grad_block, 'gy', axis=0, tiled=True)]
    unnamed x14 -> x29, local copies, waits for them, and re-layouts: 46 us -> 56 us
    unnamed x10 -> x9, waiting for transfers between devices: 60 us -> 59.8 us
  transfers between devices with their start and end apart: 9 -> 15, of which waited for: 7 -> 13; matrix products, arithmetic and copies ran while one was open for 16% -> 15% of each run, Pallas kernels for 0% -> 0%
where the time goes in v1:
time: 551 us; the launch traced here: 549 us
  waiting for transfers between devices  348 us (63%)
  matrix products  84.3 us (15%)
  local copies, waits for them, and re-layouts  56.6 us (10%)
  blocking collectives  31.6 us (6%)
  between operations  16 us (3%)
  other arithmetic  10.8 us (2%)
    psum x1, waiting for transfers between devices, per_device(): lax.psum(jnp.dot(rows_all, w_up, preferred_element_type=jnp.float32).asty...  76 us
    reduce_scatter x1, waiting for transfers between devices, per_device(): lax.psum_scatter(jnp.dot(picked, w_down, preferred_element_type=jnp.float...  63.7 us
    unnamed x9, waiting for transfers between devices  59.8 us
    unnamed x29, local copies, waits for them, and re-layouts  56 us
    ppermute x7, waiting for transfers between devices, per_device(): lax.ppermute(ring[-1], 'gy', [(dev, (dev + 1) % 8) for dev in range(8)])  53.2 us
    all_gather x1, waiting for transfers between devices, per_device(): rows_all = lax.all_gather(tokens, 'gy', axis=0, tiled=True)  45.1 us
    dot_general x5, matrix products, contract_lead(): lax.dot_general(left_mat, right_mat, (((0,), (0,)), ((), ())), preferred_...  33.1 us
    all_gather x1, blocking collectives, per_device(): proj_all = lax.all_gather(projected, 'gy', axis=0, tiled=True)  31.6 us
  transfers between devices with their start and end apart: 15, of which 13 were waited for; matrix products, arithmetic and copies ran while one was open for 15% of the time, Pallas kernels for 0%

profile of v1, /device:TPU:0, one launch (start us, length us, event | category | flops | bytes accessed | tf_op | source)
XLA Modules:
  0.0 549.2 jit_solution(2777856035686114903)
XLA Ops:
  7.9 45.1 %all-gather.4.cloned.1.call-done = bf16[256,2048]{1,0:T(8,128)(2,1)} async-done(((bf16[32,2048]{1,0:T(8,128)(2,1)}), bf16[256,2048]{1,0:T(8,128)(2,1)}) %all-gather.4.cloned.1.call-update) | async-done | bytes 1048592 | tf_op jit(solution)/shard_map/all_gather | solution.py:40
  53.0 10.8 %convolution_convert_fusion.4 = bf16[256,3584]{1,0:T(8,128)(2,1)} fusion(bf16[256,2048]{1,0:T(8,128)(2,1)} %all-gather.4.cloned.1.call-done, bf16[2048,3584]{1,0:T(8,128)(2,1)} %param.8), kind=kOutput, calls=%fused_computation.6 | convolution fusion | flops 3759013888 | bytes 17563648 | tf_op jit(solution)/shard_map/dot_general | solution.py:49
  63.8 10.3 %convolution_convert_fusion.5 = bf16[256,3584]{1,0:T(8,128)(2,1)} fusion(bf16[256,2048]{1,0:T(8,128)(2,1)S(1)} %copy-done, bf16[2048,3584]{1,0:T(8,128)(2,1)} %param.7), kind=kOutput, calls=%fused_computation.7 | convolution fusion | flops 3759013888 | bytes 17563648 | tf_op jit(solution)/shard_map/dot_general | solution.py:46
  74.1 76.0 %all-reduce.6.cloned.1.call-done = (bf16[256,3584]{1,0:T(8,128)(2,1)}, bf16[256,3584]{1,0:T(8,128)(2,1)}) async-done(((bf16[256,3584]{1,0:T(8,128)(2,1)}, bf16[256,3584]{1,0:T(8,128)(2,1)}), (bf16[256,3584]{1,0:T(8,128)(2,1)}, bf16[256,3584]{1,0:T(8,128)(2,1)})) %all-reduce.6.cloned.1.call-update) | async-done | bytes 3670032 | tf_op jit(solution)/shard_map/psum | solution.py:48
  150.1 11.6 %convolution_convert_fusion.7 = bf16[256,2048]{1,0:T(8,128)(2,1)} fusion(bf16[3584,2048]{1,0:T(8,128)(2,1)} %param.9, bf16[256,3584]{1,0:T(8,128)(2,1)} %get-tuple-element.20, bf16[256,3584]{1,0:T(8,128)(2,1)} %get-tuple-element.21), kind=kOutput, calls=%fused_computation.10 | convolution fusion | flops 3765960704 | bytes 19398656 | tf_op jit(solution)/shard_map/dot_general | solution.py:57
  161.8 63.7 %reduce-scatter.6.cloned.1.call-done = bf16[32,2048]{1,0:T(8,128)(2,1)} async-done(((bf16[256,2048]{1,0:T(8,128)(2,1)}), bf16[32,2048]{1,0:T(8,128)(2,1)}) %reduce-scatter.6.cloned.1.call-update) | async-done | bytes 131088 | tf_op jit(solution)/shard_map/reduce_scatter | solution.py:56
  230.3 30.2 %all-reduce.4.cloned.1.call-done = bf16[32,1024]{1,0:T(8,128)(2,1)} async-done(((bf16[32,1024]{1,0:T(8,128)(2,1)}), bf16[32,1024]{1,0:T(8,128)(2,1)}) %all-reduce.4.cloned.1.call-update) | async-done | bytes 65552 | tf_op jit(solution)/shard_map/psum | solution.py:63
  260.4 31.6 %all_gather.13 = bf16[256,1024]{1,0:T(8,128)(2,1)S(1)} all-gather(bf16[32,1024]{1,0:T(8,128)(2,1)} %all-reduce.4.cloned.1.call-done), channel_id=1, replica_groups=mesh['gx'=4,'gy'=8] {'gy'}, dimensions={0}, use_global_device_ids=true | all-gather | bytes 589824 | tf_op jit(solution)/shard_map/all_gather | solution.py:66
  298.6 6.2 %collective-permute-done = bf16[32,2048]{1,0:T(8,128)(2,1)S(1)} collective-permute-done((bf16[32,2048]{1,0:T(8,128)(2,1)S(1)}, bf16[32,2048]{1,0:T(8,128)(2,1)S(1)}, u32[]{:S(2)}, u32[]{:S(2)}) %collective-permute-start) | collective-permute-done | bytes 131104 | tf_op jit(solution)/shard_map/ppermute | solution.py:84
  304.8 7.7 %collective-permute-done.1 = bf16[32,2048]{1,0:T(8,128)(2,1)S(1)} collective-permute-done((bf16[32,2048]{1,0:T(8,128)(2,1)S(1)}, bf16[32,2048]{1,0:T(8,128)(2,1)S(1)}, u32[]{:S(2)}, u32[]{:S(2)}) %collective-permute-start.1) | collective-permute-done | bytes 131104 | tf_op jit(solution)/shard_map/ppermute | solution.py:84
  312.5 7.7 %collective-permute-done.2 = bf16[32,2048]{1,0:T(8,128)(2,1)S(1)} collective-permute-done((bf16[32,2048]{1,0:T(8,128)(2,1)S(1)}, bf16[32,2048]{1,0:T(8,128)(2,1)S(1)}, u32[]{:S(2)}, u32[]{:S(2)}) %collective-permute-start.2) | collective-permute-done | bytes 131104 | tf_op jit(solution)/shard_map/ppermute | solution.py:84
  320.2 7.7 %collective-permute-done.3 = bf16[32,2048]{1,0:T(8,128)(2,1)S(1)} collective-permute-done((bf16[32,2048]{1,0:T(8,128)(2,1)S(1)}, bf16[32,2048]{1,0:T(8,128)(2,1)S(1)}, u32[]{:S(2)}, u32[]{:S(2)}) %collective-permute-start.3) | collective-permute-done | bytes 131104 | tf_op jit(solution)/shard_map/ppermute | solution.py:84
  327.8 8.7 %collective-permute-done.4 = bf16[32,2048]{1,0:T(8,128)(2,1)S(1)} collective-permute-done((bf16[32,2048]{1,0:T(8,128)(2,1)S(1)}, bf16[32,2048]{1,0:T(8,128)(2,1)S(1)}, u32[]{:S(2)}, u32[]{:S(2)}) %collective-permute-start.4) | collective-permute-done | bytes 131104 | tf_op jit(solution)/shard_map/ppermute | solution.py:84
  336.6 7.7 %collective-permute-done.5 = bf16[32,2048]{1,0:T(8,128)(2,1)S(1)} collective-permute-done((bf16[32,2048]{1,0:T(8,128)(2,1)S(1)}, bf16[32,2048]{1,0:T(8,128)(2,1)S(1)}, u32[]{:S(2)}, u32[]{:S(2)}) %collective-permute-start.5) | collective-permute-done | bytes 131104 | tf_op jit(solution)/shard_map/ppermute | solution.py:84
  344.2 7.7 %collective-permute-done.6 = bf16[32,2048]{1,0:T(8,128)(2,1)S(1)} collective-permute-done((bf16[32,2048]{1,0:T(8,128)(2,1)S(1)}, bf16[32,2048]{1,0:T(8,128)(2,1)S(1)}, u32[]{:S(2)}, u32[]{:S(2)}) %collective-permute-start.6) | collective-permute-done | bytes 131104 | tf_op jit(solution)/shard_map/ppermute | solution.py:84
  362.5 10.7 %convolution_convert_fusion.3 = bf16[256,3584]{1,0:T(8,128)(2,1)} fusion(bf16[3584,2048]{1,0:T(8,128)(2,1)} %param.9, bf16[512,2048]{1,0:T(8,128)(2,1)} %constant_dynamic-update-slice_fusion, s32[]{:T(128)S(6)} %select_n.33), kind=kOutput, calls=%fused_computation.5 | convolution fusion | flops 3759013888 | bytes 17563652 | tf_op jit(solution)/shard_map/dot_general | solution.py:15
  379.6 20.0 %reduce-scatter.8.cloned.1.call-done = bf16[64,3584]{1,0:T(8,128)(2,1)} async-done(((bf16[256,3584]{1,0:T(8,128)(2,1)}), bf16[64,3584]{1,0:T(8,128)(2,1)}) %reduce-scatter.8.cloned.1.call-update) | async-done | bytes 458768 | tf_op jit(solution)/shard_map/reduce_scatter | solution.py:90
  406.6 6.5 %copy.16 = bf16[2048,1024]{0,1:T(8,128)(2,1)} copy(bf16[2048,1024]{1,0:T(8,128)(2,1)} %convolution_convert_fusion.6) | data formatting | bytes 8388608
  413.8 11.7 %convolution_convert_fusion = bf16[3584,2048]{1,0:T(8,128)(2,1)} fusion(bf16[512,2048]{1,0:T(8,128)(2,1)} %constant_dynamic-update-slice_fusion, s32[]{:T(128)S(6)} %select_n.33, bf16[256,3584]{1,0:T(8,128)(2,1)S(1)} %copy-done.1, bf16[256,3584]{1,0:T(8,128)(2,1)} %get-tuple-element.21), kind=kOutput, calls=%fused_computation | convolution fusion | flops 3772776448 | bytes 19398660 | tf_op jit(solution)/shard_map/dot_general | solution.py:9
  425.5 9.1 %fusion = bf16[2048,3584]{0,1:T(8,128)(2,1)} fusion(bf16[256,3584]{1,0:T(8,128)(2,1)} %all-gather.6.cloned.1.call-done, bf16[256,2048]{1,0:T(8,128)(2,1)S(1)} %copy-done), kind=kOutput, calls=%fused_computation.3 | convolution fusion | flops 3765436416 | bytes 17563648 | tf_op jit(solution)/shard_map/dot_general | solution.py:9
  434.6 18.7 %copy.14 = bf16[2048,3584]{1,0:T(8,128)(2,1)} copy(bf16[2048,3584]{0,1:T(8,128)(2,1)} %fusion) | data formatting | bytes 29360128
  453.3 8.8 %fusion.1 = bf16[2048,3584]{0,1:T(8,128)(2,1)} fusion(bf16[256,3584]{1,0:T(8,128)(2,1)} %all-gather.8.cloned.1.call-done, bf16[256,2048]{1,0:T(8,128)(2,1)S(1)} %copy-done), kind=kOutput, calls=%fused_computation.4 | convolution fusion | flops 3765436416 | bytes 17563648 | tf_op jit(solution)/shard_map/dot_general | solution.py:9
  462.0 18.8 %copy.15 = bf16[2048,3584]{1,0:T(8,128)(2,1)} copy(bf16[2048,3584]{0,1:T(8,128)(2,1)} %fusion.1) | data formatting | bytes 29360128
  480.8 58.4 %reduce-scatter.10.cloned.1.call-done = bf16[128,2048]{1,0:T(8,128)(2,1)} async-done(((bf16[1024,2048]{1,0:T(8,128)(2,1)}), bf16[128,2048]{1,0:T(8,128)(2,1)}) %reduce-scatter.10.cloned.1.call-update) | async-done | bytes 524304
  (65 shorter events, 38.2 us)
Async XLA Ops:
  7.2 45.8 %all-gather.4.cloned.1.call-start = ((), (), s32[]{:S(2)}) async-start(), calls=%async_computation.3 | async-start | bytes 1179648 | tf_op jit(solution)/shard_map/all_gather | solution.py:40
  7.9 142.2 %all-reduce.6.cloned.1.call-start = ((), (), s32[]{:S(2)}) async-start(), calls=%async_computation.10 | async-start | bytes 7340032 | tf_op jit(solution)/shard_map/psum | solution.py:48
  53.0 10.8 %copy-start = (bf16[256,2048]{1,0:T(8,128)(2,1)S(1)}, bf16[256,2048]{1,0:T(8,128)(2,1)}, u32[]{:S(2)}) copy-start(bf16[256,2048]{1,0:T(8,128)(2,1)} %all-gather.4.cloned.1.call-done) | copy-start | bytes 3145732
  74.1 151.5 %reduce-scatter.6.cloned.1.call-start = ((), (), s32[]{:S(2)}) async-start(), calls=%async_computation.4 | async-start | bytes 1179648 | tf_op jit(solution)/shard_map/reduce_scatter | solution.py:56
  150.1 75.4 %copy-start.3 = (bf16[32,2048]{1,0:T(8,128)(2,1)S(1)}, bf16[32,2048]{1,0:T(8,128)(2,1)}, u32[]{:S(2)}) copy-start(bf16[32,2048]{1,0:T(8,128)(2,1)} %param.6) | copy-start | bytes 393220
  161.7 98.7 %all-reduce.4.cloned.1.call-start = ((), (), s32[]{:S(2)}) async-start(), calls=%async_computation.5 | async-start | bytes 131072 | tf_op jit(solution)/shard_map/psum | solution.py:63
  226.5 176.9 %copy-start.2 = (bf16[32,2048]{1,0:T(8,128)(2,1)}, bf16[32,2048]{1,0:T(8,128)(2,1)S(1)}, u32[]{:S(2)}) copy-start(bf16[32,2048]{1,0:T(8,128)(2,1)S(1)} %add_convert_fusion) | copy-start | bytes 393220
  226.5 65.9 %copy-start.4 = (s32[256]{0:T(256)S(1)}, s32[256]{0:T(256)}, u32[]{:S(2)}) copy-start(s32[256]{0:T(256)} %param.11) | copy-start | bytes 3076
  230.2 169.3 %reduce-scatter.8.cloned.1.call-start = ((), (), s32[]{:S(2)}) async-start(), calls=%async_computation.6 | async-start | bytes 2293760 | tf_op jit(solution)/shard_map/reduce_scatter | solution.py:90
  297.2 7.7 %collective-permute-start = (bf16[32,2048]{1,0:T(8,128)(2,1)S(1)}, bf16[32,2048]{1,0:T(8,128)(2,1)S(1)}, u32[]{:S(2)}, u32[]{:S(2)}) collective-permute-start(bf16[32,2048]{1,0:T(8,128)(2,1)S(1)} %convolution_convert_fusion.8), channel_id=1, source_target_pairs={{0,1},{1,2},{2,3},{3,4},{4,5},{5,6},{6,7},{7,0},{8,9},{9,10},{10,1... | collective-permute-start | bytes 393224 | tf_op jit(solution)/shard_map/ppermute | solution.py:84
  304.8 7.7 %collective-permute-start.1 = (bf16[32,2048]{1,0:T(8,128)(2,1)S(1)}, bf16[32,2048]{1,0:T(8,128)(2,1)S(1)}, u32[]{:S(2)}, u32[]{:S(2)}) collective-permute-start(bf16[32,2048]{1,0:T(8,128)(2,1)S(1)} %collective-permute-done), channel_id=1, source_target_pairs={{0,1},{1,2},{2,3},{3,4},{4,5},{5,6},{6,7},{7,0},{8,9},{9,10},{10,1... | collective-permute-start | bytes 393224 | tf_op jit(solution)/shard_map/ppermute | solution.py:84
  312.5 7.7 %collective-permute-start.2 = (bf16[32,2048]{1,0:T(8,128)(2,1)S(1)}, bf16[32,2048]{1,0:T(8,128)(2,1)S(1)}, u32[]{:S(2)}, u32[]{:S(2)}) collective-permute-start(bf16[32,2048]{1,0:T(8,128)(2,1)S(1)} %collective-permute-done.1), channel_id=1, source_target_pairs={{0,1},{1,2},{2,3},{3,4},{4,5},{5,6},{6,7},{7,0},{8,9},{9,10},{10,1... | collective-permute-start | bytes 393224 | tf_op jit(solution)/shard_map/ppermute | solution.py:84
  320.2 7.7 %collective-permute-start.3 = (bf16[32,2048]{1,0:T(8,128)(2,1)S(1)}, bf16[32,2048]{1,0:T(8,128)(2,1)S(1)}, u32[]{:S(2)}, u32[]{:S(2)}) collective-permute-start(bf16[32,2048]{1,0:T(8,128)(2,1)S(1)} %collective-permute-done.2), channel_id=1, source_target_pairs={{0,1},{1,2},{2,3},{3,4},{4,5},{5,6},{6,7},{7,0},{8,9},{9,10},{10,1... | collective-permute-start | bytes 393224 | tf_op jit(solution)/shard_map/ppermute | solution.py:84
  327.8 8.7 %collective-permute-start.4 = (bf16[32,2048]{1,0:T(8,128)(2,1)S(1)}, bf16[32,2048]{1,0:T(8,128)(2,1)S(1)}, u32[]{:S(2)}, u32[]{:S(2)}) collective-permute-start(bf16[32,2048]{1,0:T(8,128)(2,1)S(1)} %collective-permute-done.3), channel_id=1, source_target_pairs={{0,1},{1,2},{2,3},{3,4},{4,5},{5,6},{6,7},{7,0},{8,9},{9,10},{10,1... | collective-permute-start | bytes 393224 | tf_op jit(solution)/shard_map/ppermute | solution.py:84
  336.6 7.7 %collective-permute-start.5 = (bf16[32,2048]{1,0:T(8,128)(2,1)S(1)}, bf16[32,2048]{1,0:T(8,128)(2,1)S(1)}, u32[]{:S(2)}, u32[]{:S(2)}) collective-permute-start(bf16[32,2048]{1,0:T(8,128)(2,1)S(1)} %collective-permute-done.4), channel_id=1, source_target_pairs={{0,1},{1,2},{2,3},{3,4},{4,5},{5,6},{6,7},{7,0},{8,9},{9,10},{10,1... | collective-permute-start | bytes 393224 | tf_op jit(solution)/shard_map/ppermute | solution.py:84
  344.2 7.7 %collective-permute-start.6 = (bf16[32,2048]{1,0:T(8,128)(2,1)S(1)}, bf16[32,2048]{1,0:T(8,128)(2,1)S(1)}, u32[]{:S(2)}, u32[]{:S(2)}) collective-permute-start(bf16[32,2048]{1,0:T(8,128)(2,1)S(1)} %collective-permute-done.5), channel_id=1, source_target_pairs={{0,1},{1,2},{2,3},{3,4},{4,5},{5,6},{6,7},{7,0},{8,9},{9,10},{10,1... | collective-permute-start | bytes 393224 | tf_op jit(solution)/shard_map/ppermute | solution.py:84
  373.3 52.2 %all-gather.6.cloned.1.call-start = ((), (), s32[]{:S(2)}) async-start(), calls=%async_computation.7 | async-start | bytes 2293760 | tf_op jit(solution)/shard_map/all_gather | solution.py:99
  373.4 3.9 copy-start.1
  402.5 50.8 %all-gather.8.cloned.1.call-start = ((), (), s32[]{:S(2)}) async-start(), calls=%async_computation.8 | async-start | bytes 2293760 | tf_op jit(solution)/shard_map/all_gather | solution.py:100
  403.3 135.9 %reduce-scatter.10.cloned.1.call-start = ((), (), s32[]{:S(2)}) async-start(), calls=%async_computation.9 | async-start | bytes 4718592
Sparse Core Ops, SparseCore 0:
  10.1 42.8 all-gather.3
  74.2 75.9 all-reduce.5
  161.9 63.6 reduce-scatter.5
  230.3 30.0 all-reduce.3
  373.4 26.0 reduce-scatter.7
  402.6 21.1 all-gather.5
  426.0 21.1 all-gather.7
  451.2 87.9 reduce-scatter.9
